TPU v7x, 32 devices: a whole 2x2x4 slice. The times are simulated.
32 devices in a mesh: ctx: 8 (over y, x, core), ch: 4 (over z).
Axes of the slice: x: 2, y: 2, z: 4, core: 2. Of those that a mesh axis runs over, the one named last changes fastest.
Arguments:
- queries: bfloat16 [8192, 2048], P('ch', 'ctx'), may hold values from -6 to 6
- keys: bfloat16 [8192, 2048], P('ch', 'ctx'), may hold values from -6 to 6
- values: bfloat16 [8192, 2048], P('ch', 'ctx'), may hold values from -6 to 6
- short_taps: float32 [3, 7, 8192], P(None, None, 'ch'), may hold values from -2 to 2
- long_filter: bfloat16 [4, 2048, 2048], P('ch', 'ctx'), may hold values from -1.5 to 1.5
- skip_gain: float32 [4, 2048], P('ch', 'ctx'), may hold values from 0.5 to 1.5
Outputs:
- mixed: bfloat16 [8192, 2048], P('ch', 'ctx')
All inputs are finite; a program needn't handle non-finite values.
Results may differ from a plain program's by a relative error of at most 0.01.
Values may be sent and summed in bfloat16 or wider, within the bound.
A program may use at most 64 MiB of HBM per device.

v0:
```python
import math
import jax
import jax.numpy as jnp
from jax import lax
from jax.sharding import PartitionSpec as P

HIGH = lax.Precision.HIGHEST


def passed_along(value, axis, by):
    peers = lax.axis_size(axis)
    pairs = [(i, i + by) for i in range(peers) if 0 <= i + by < peers]
    return lax.ppermute(value, axis, pairs)


def short_conv(extended, taps, length):
    rim = taps.shape[0] - 1
    total = jnp.zeros((extended.shape[0], length), jnp.float32)
    for shift_j in range(taps.shape[0]):
        total = total + taps[shift_j][:, None] * extended[:, rim - shift_j : rim - shift_j + length]
    return total


def split_table(table):
    table_head = table.astype(jnp.bfloat16)
    table_rest = (table - table_head.astype(jnp.float32)).astype(jnp.bfloat16)
    return (table_head, table_rest)


def long_conv(gated, filters, skips):
    channels, length = gated.shape
    size = 2 * length
    cols = 128
    rows = size // cols
    half = rows // 2
    two_pi = 2.0 * math.pi
    row_idx = jnp.arange(rows, dtype=jnp.int32)
    half_idx = jnp.arange(half, dtype=jnp.int32)
    col_idx = jnp.arange(cols, dtype=jnp.int32)
    angle_rows = two_pi * (row_idx[:, None] * half_idx[None, :] % rows).astype(jnp.float32) / rows
    cos_rows, sin_rows = (jnp.cos(angle_rows), jnp.sin(angle_rows))
    cos_head, cos_rest = split_table(cos_rows)
    sin_head, sin_rest = split_table(sin_rows)
    angle_twist = two_pi * (row_idx[:, None] * col_idx[None, :]).astype(jnp.float32) / size
    cos_twist, sin_twist = (jnp.cos(angle_twist), jnp.sin(angle_twist))
    angle_cols = two_pi * (col_idx[:, None] * col_idx[None, :] % cols).astype(jnp.float32) / cols
    cos_cols, sin_cols = (jnp.cos(angle_cols), jnp.sin(angle_cols))

    def first_section(table_head, table_rest, shaped):
        return jnp.einsum(
            "ka,cab->ckb", table_head, shaped, preferred_element_type=jnp.float32
        ) + jnp.einsum("ka,cab->ckb", table_rest, shaped, preferred_element_type=jnp.float32)

    def forward(signal):
        blocks = signal.shape[0]
        shaped = signal.reshape(blocks, half, cols)
        first_re = first_section(cos_head, cos_rest, shaped)
        first_im = -first_section(sin_head, sin_rest, shaped)
        twist_re = first_re * cos_twist + first_im * sin_twist
        twist_im = first_im * cos_twist - first_re * sin_twist
        out_re = jnp.einsum("ckb,bm->ckm", twist_re, cos_cols, precision=HIGH) + jnp.einsum(
            "ckb,bm->ckm", twist_im, sin_cols, precision=HIGH
        )
        out_im = jnp.einsum("ckb,bm->ckm", twist_im, cos_cols, precision=HIGH) - jnp.einsum(
            "ckb,bm->ckm", twist_re, sin_cols, precision=HIGH
        )
        return (out_re, out_im)

    def inverse(spec_re, spec_im):
        blocks = spec_re.shape[0]
        back_re = jnp.einsum("ckm,mb->ckb", spec_re, cos_cols, precision=HIGH) - jnp.einsum(
            "ckm,mb->ckb", spec_im, sin_cols, precision=HIGH
        )
        back_im = jnp.einsum("ckm,mb->ckb", spec_im, cos_cols, precision=HIGH) + jnp.einsum(
            "ckm,mb->ckb", spec_re, sin_cols, precision=HIGH
        )
        turn_re = back_re * cos_twist - back_im * sin_twist
        turn_im = back_re * sin_twist + back_im * cos_twist
        result = jnp.einsum("ka,ckb->cab", cos_rows, turn_re, precision=HIGH) - jnp.einsum(
            "ka,ckb->cab", sin_rows, turn_im, precision=HIGH
        )
        return (result / size).reshape(blocks, length)

    block = math.gcd(channels, 16)
    count = channels // block

    def one_block(triple):
        sig, filt, gain = triple
        sig_re, sig_im = forward(sig)
        filt_re, filt_im = forward(filt)
        prod_re = sig_re * filt_re - sig_im * filt_im
        prod_im = sig_re * filt_im + sig_im * filt_re
        return inverse(prod_re, prod_im) + gain[:, None] * sig.astype(jnp.float32)

    outcome = lax.map(
        one_block,
        (
            gated.reshape(count, block, length),
            filters.reshape(count, block, length),
            skips.reshape(count, block),
        ),
    )
    return outcome.reshape(channels, length).astype(jnp.bfloat16)


def gate_product(first, second):
    return (first.astype(jnp.float32) * second.astype(jnp.float32)).astype(jnp.bfloat16)


def local(queries, keys, values, short_taps, long_filter, skip_gain):
    width, tok_local = queries.shape
    rim = short_taps.shape[1] - 1
    stacked = jnp.stack(
        [queries[:, tok_local - rim :], keys[:, tok_local - rim :], values[:, tok_local - rim :]]
    )
    before = passed_along(stacked, "ctx", 1)

    def extend_home(source, which):
        return jnp.concatenate([before[which], source], axis=1).astype(jnp.float32)

    q_short = short_conv(extend_home(queries, 0), short_taps[0], tok_local).astype(jnp.bfloat16)
    gated = (
        short_conv(extend_home(keys, 1), short_taps[1], tok_local)
        * short_conv(extend_home(values, 2), short_taps[2], tok_local)
    ).astype(jnp.bfloat16)
    g_owned = lax.all_to_all(gated, "ctx", split_axis=0, concat_axis=1, tiled=True)
    outgoing = long_conv(g_owned, long_filter[0], skip_gain[0])
    returned = lax.all_to_all(outgoing, "ctx", split_axis=1, concat_axis=0, tiled=True)
    return gate_product(q_short, returned)


def solution(mesh):
    placed = (
        P("ch", "ctx"),
        P("ch", "ctx"),
        P("ch", "ctx"),
        P(None, None, "ch"),
        P("ch", "ctx", None),
        P("ch", "ctx"),
    )
    return jax.shard_map(
        local, mesh=mesh, in_specs=placed, out_specs=P("ch", "ctx"), check_vma=False
    )
```

profile of v0, /device:TPU:0, one launch (start us, length us, event | category | flops | bytes accessed | tf_op | source)
XLA Modules:
  0.0 269.8 jit_solution(2288781871409935307)
XLA Ops:
  0.0 1.3 slice.190
  1.6 1.3 slice.191
  3.5 2.4 collective-permute-start
  6.1 0.8 collective-permute-done
  7.5 1.3 maximum_convert_fusion.1
  8.8 11.8 %fusion.204 = bf16[2048,256]{1,0:T(8,128)(2,1)} fusion(f32[2048,262]{1,0:T(8,128)S(1)} %get-tuple-element.288, f32[2048,262]{1,0:T(8,128)S(1)} %get-tuple-element.287, f32[2048]{0:T(1024)S(1)} %bitcast.245, f32[2048]{0:T(1024)S(1)} %bitcast.244, f32[2048]{0:T(1024)S(1)} %bitcast.233, f32[2048]{0:T(1024)S(1)} %bitcast.234, f32[2048]{0:T(1024)S(1)} %bitcast.235, ...), kind=kLoop, calls=%fused_computation.203 | loop fusion | flops 14680064 | bytes 30523392 | tf_op jit(solution)/shard_map/convert_element_type | solution.py:125
  20.6 7.9 %all-to-all-start = ((bf16[8,256,256]{2,1,0:T(8,128)(2,1)}), bf16[8,256,256]{2,1,0:T(8,128)(2,1)S(1)}, u32[]{:S(2)}, u32[]{:S(2)}) async-start(bf16[8,256,256]{2,1,0:T(8,128)(2,1)} %bitcast.27), calls=%async_computation | async-start | bytes 2097152 | tf_op jit(solution)/shard_map/all_to_all | solution.py:126
  29.1 0.7 reduce.3
  29.9 14.0 %all-to-all-done = bf16[8,256,256]{2,1,0:T(8,128)(2,1)S(1)} async-done(((bf16[8,256,256]{2,1,0:T(8,128)(2,1)}), bf16[8,256,256]{2,1,0:T(8,128)(2,1)S(1)}, u32[]{:S(2)}, u32[]{:S(2)}) %all-to-all-start) | async-done | bytes 1048608 | tf_op jit(solution)/shard_map/all_to_all | solution.py:126
  45.0 195.2 %while.12 = (s32[]{:T(128)}, bf16[16,16,2048]{2,1,0:T(8,128)(2,1)}, bf16[16,16,2048]{2,1,0:T(8,128)(2,1)S(1)}, bf16[16,16,2048]{2,1,0:T(8,128)(2,1)}, f32[16,16]{1,0:T(8,128)S(1)}, /*index=5*/s32[]{:T(128)}) while((s32[]{:T(128)}, bf16[16,16,2048]{2,1,0:T(8,128)(2,1)}, bf16[16,16,2048]{2,1,0:T(8,128)(2,1)S(1)}, ...), condition=%wide.region_1.2_spmd.clone.clone, body=%wide.region_0.1_spmd.clone.clone.sunk | while | flops 1256058880 | bytes 17597196 | solution.py:95
  45.1 0.9 dynamic-slice_bitcast_fusion.3
  52.6 0.6 multiply_subtract_fusion.16
  56.5 0.7 add_dynamic-update-slice_fusion.2
  57.2 0.8 dynamic-slice_bitcast_fusion.3
  64.8 0.7 multiply_subtract_fusion.16
  68.7 0.7 add_dynamic-update-slice_fusion.2
  69.5 0.8 dynamic-slice_bitcast_fusion.3
  80.9 0.7 add_dynamic-update-slice_fusion.2
  81.6 0.8 dynamic-slice_bitcast_fusion.3
  89.2 0.7 multiply_subtract_fusion.16
  93.1 0.7 add_dynamic-update-slice_fusion.2
  93.8 0.8 dynamic-slice_bitcast_fusion.3
  101.4 0.6 multiply_subtract_fusion.16
  105.3 0.7 add_dynamic-update-slice_fusion.2
  106.0 0.8 dynamic-slice_bitcast_fusion.3
  113.6 0.7 multiply_subtract_fusion.16
  117.5 0.7 add_dynamic-update-slice_fusion.2
  118.2 0.8 dynamic-slice_bitcast_fusion.3
  125.8 0.6 multiply_subtract_fusion.16
  129.7 0.7 add_dynamic-update-slice_fusion.2
  130.4 0.8 dynamic-slice_bitcast_fusion.3
  138.0 0.7 multiply_subtract_fusion.16
  141.9 0.7 add_dynamic-update-slice_fusion.2
  142.6 0.8 dynamic-slice_bitcast_fusion.3
  150.2 0.6 multiply_subtract_fusion.16
  154.1 0.7 add_dynamic-update-slice_fusion.2
  154.8 0.8 dynamic-slice_bitcast_fusion.3
  162.4 0.7 multiply_subtract_fusion.16
  166.3 0.7 add_dynamic-update-slice_fusion.2
  167.0 0.8 dynamic-slice_bitcast_fusion.3
  174.6 0.6 multiply_subtract_fusion.16
  178.5 0.7 add_dynamic-update-slice_fusion.2
  179.2 0.8 dynamic-slice_bitcast_fusion.3
  186.8 0.7 multiply_subtract_fusion.16
  190.7 0.7 add_dynamic-update-slice_fusion.2
  191.4 0.8 dynamic-slice_bitcast_fusion.3
  199.0 0.6 multiply_subtract_fusion.16
  202.9 0.7 add_dynamic-update-slice_fusion.2
  203.6 0.8 dynamic-slice_bitcast_fusion.3
  211.2 0.7 multiply_subtract_fusion.16
  215.1 0.7 add_dynamic-update-slice_fusion.2
  215.8 0.8 dynamic-slice_bitcast_fusion.3
  223.4 0.6 multiply_subtract_fusion.16
  227.3 0.7 add_dynamic-update-slice_fusion.2
  228.0 0.8 dynamic-slice_bitcast_fusion.3
  235.6 0.7 multiply_subtract_fusion.16
  239.5 0.7 add_dynamic-update-slice_fusion.2
  240.2 1.5 copy.29
  241.8 1.2 copy.23
  242.9 4.2 %all-to-all-start.1 = ((bf16[256,8,256]{2,0,1:T(8,128)(2,1)}), bf16[256,8,256]{2,0,1:T(8,128)(2,1)}, u32[]{:S(2)}, u32[]{:S(2)}) async-start(bf16[256,8,256]{2,0,1:T(8,128)(2,1)} %copy.23), calls=%async_computation.1 | async-start | bytes 2097152 | tf_op jit(solution)/shard_map/all_to_all | solution.py:128
  247.2 1.1 copy.19
  248.3 2.0 maximum_convert_fusion
  250.3 12.3 %all-to-all-done.1 = bf16[256,8,256]{2,0,1:T(8,128)(2,1)} async-done(((bf16[256,8,256]{2,0,1:T(8,128)(2,1)}), bf16[256,8,256]{2,0,1:T(8,128)(2,1)}, u32[]{:S(2)}, u32[]{:S(2)}) %all-to-all-start.1) | async-done | bytes 1048608 | tf_op jit(solution)/shard_map/all_to_all | solution.py:128
  262.6 7.2 %fusion.223 = bf16[2048,256]{1,0:T(8,128)(2,1)} fusion(f32[2048,262]{1,0:T(8,128)S(1)} %maximum_convert_fusion, f32[2048]{0:T(1024)S(1)} %bitcast.225, f32[2048]{0:T(1024)S(1)} %bitcast.226, f32[2048]{0:T(1024)S(1)} %bitcast.227, f32[2048]{0:T(1024)S(1)} %bitcast.228, f32[2048]{0:T(1024)S(1)} %bitcast.229, f32[2048]{0:T(1024)S(1)} %bitcast.230, ...), kind=kLoop, calls=%fused_computation.243 | loop fusion | flops 9437184 | bytes 16834560 | tf_op jit(solution)/shard_map/convert_element_type | solution.py:107
  (440 shorter events, 160.5 us)
Async XLA Ops:
  0.0 3.1 %copy-start = (bf16[2048,256]{1,0:T(8,128)(2,1)S(1)}, bf16[2048,256]{1,0:T(8,128)(2,1)}, u32[]{:S(2)}) copy-start(bf16[2048,256]{1,0:T(8,128)(2,1)} %param.10) | copy-start | bytes 3145732
  1.3 4.6 %copy-start.2 = (f32[3,7,2048]{2,1,0:T(8,128)S(1)}, f32[3,7,2048]{2,1,0:T(8,128)}, u32[]{:S(2)}) copy-start(f32[3,7,2048]{2,1,0:T(8,128)} %param.11) | copy-start | bytes 516100
  2.8 4.7 %copy-start.1 = (bf16[2048,256]{1,0:T(8,128)(2,1)S(1)}, bf16[2048,256]{1,0:T(8,128)(2,1)}, u32[]{:S(2)}) copy-start(bf16[2048,256]{1,0:T(8,128)(2,1)} %param.9) | copy-start | bytes 3145732
  3.5 3.3 %collective-permute-start = (bf16[3,2048,6]{1,2,0:T(8,128)(2,1)S(1)}, bf16[3,2048,6]{1,2,0:T(8,128)(2,1)S(1)}, u32[]{:S(2)}, u32[]{:S(2)}) collective-permute-start(bf16[3,2048,6]{1,2,0:T(8,128)(2,1)S(1)} %pad_maximum_fusion), channel_id=1, source_target_pairs={{0,4},{4,8},{8,12},{12,16},{16,20},{20,24},{24,28},{1,5},{5,9},{9,... | collective-permute-start | bytes 221192 | tf_op jit(solution)/shard_map/ppermute | solution.py:13
  20.6 8.5 %copy-start.3 = (f32[1,256]{1,0:T(1,128)S(1)}, f32[1,256]{1,0:T(1,128)}, u32[]{:S(2)}) copy-start(f32[1,256]{1,0:T(1,128)} %param.13) | copy-start | bytes 3076
  20.6 23.3 %all-to-all-start = ((bf16[8,256,256]{2,1,0:T(8,128)(2,1)}), bf16[8,256,256]{2,1,0:T(8,128)(2,1)S(1)}, u32[]{:S(2)}, u32[]{:S(2)}) async-start(bf16[8,256,256]{2,1,0:T(8,128)(2,1)} %bitcast.27), calls=%async_computation | async-start | bytes 2097152 | tf_op jit(solution)/shard_map/all_to_all | solution.py:126
  242.9 19.6 %all-to-all-start.1 = ((bf16[256,8,256]{2,0,1:T(8,128)(2,1)}), bf16[256,8,256]{2,0,1:T(8,128)(2,1)}, u32[]{:S(2)}, u32[]{:S(2)}) async-start(bf16[256,8,256]{2,0,1:T(8,128)(2,1)} %copy.23), calls=%async_computation.1 | async-start | bytes 2097152 | tf_op jit(solution)/shard_map/all_to_all | solution.py:128
where the time goes:
time: 271 us; the launch traced here: 270 us
  matrix products  164 us (61%)
  other arithmetic  35.8 us (13%)
  waiting for transfers between devices  27 us (10%)
  local copies, waits for them, and re-layouts  24.4 us (9%)
  starting transfers between devices  14.6 us (5%)
  loops' own time  3.38 us (1%)
    dot_general x32, matrix products, forward(): jnp.einsum('ckb,bm->ckm', twist_re, sin_cols, precision=HIGH)  20.2 us
    dot_general x32, matrix products, forward(): jnp.einsum('ckb,bm->ckm', twist_im, sin_cols, precision=HIGH)  19.7 us
    dot_general x32, matrix products, forward(): jnp.einsum('ckb,bm->ckm', twist_im, cos_cols, precision=HIGH)  19.5 us
    dot_general x32, matrix products, forward(): jnp.einsum('ckb,bm->ckm', twist_re, cos_cols, precision=HIGH)  19.5 us
    dot_general x64, matrix products, first_section(): jnp.einsum('ka,cab->ckb', table_rest, shaped, preferred_element_type=jnp....  17.9 us
    dot_general x64, matrix products, first_section(): jnp.einsum('ka,cab->ckb', table_head, shaped, preferred_element_type=jnp....  17.5 us
    all_to_all x1, waiting for transfers between devices, local(): lax.all_to_all(gated, 'ctx', split_axis=0, concat_axis=1, tiled=True)  14 us
    while x48, local copies, waits for them, and re-layouts  14 us
  transfers between devices with their start and end apart: 3, of which 3 were waited for; matrix products, arithmetic and copies ran while one was open for 2% of the time, Pallas kernels for 0%

commit v1 on v0

--- a/solution.py
+++ b/solution.py
@@ -5,6 +5,29 @@
 from jax.sharding import PartitionSpec as P
 
 HIGH = lax.Precision.HIGHEST
+
+
+def in_blocks(x, dim, count):
+    shape = x.shape
+    blocks = x.reshape(*shape[:dim], count, shape[dim] // count, *shape[dim + 1 :])
+    return jnp.moveaxis(blocks, dim, 0)
+
+
+def in_order(tiles, dim):
+    tiles = jnp.moveaxis(tiles, 0, dim)
+    shape = tiles.shape
+    return tiles.reshape(*shape[:dim], shape[dim] * shape[dim + 1], *shape[dim + 2 :])
+
+
+def exchange_directly(shard, axis, split_dim, concat_dim):
+    size, index = (lax.axis_size(axis), lax.axis_index(axis))
+    blocks = in_blocks(shard, split_dim, size)
+    finished = [blocks[index]]
+    for step in range(1, size):
+        sent = blocks[(index + step) % size]
+        finished.append(lax.ppermute(sent, axis, [(i, (i + step) % size) for i in range(size)]))
+    blocks = jnp.stack(finished)[(index - jnp.arange(size)) % size]
+    return in_order(blocks, concat_dim)
 
 
 def passed_along(value, axis, by):
@@ -123,7 +146,7 @@
         short_conv(extend_home(keys, 1), short_taps[1], tok_local)
         * short_conv(extend_home(values, 2), short_taps[2], tok_local)
     ).astype(jnp.bfloat16)
-    g_owned = lax.all_to_all(gated, "ctx", split_axis=0, concat_axis=1, tiled=True)
+    g_owned = exchange_directly(gated, "ctx", 0, 1)
     outgoing = long_conv(g_owned, long_filter[0], skip_gain[0])
     returned = lax.all_to_all(outgoing, "ctx", split_axis=1, concat_axis=0, tiled=True)
     return gate_product(q_short, returned)

time: 271 us -> 257 us (0.948)
  other arithmetic: 35.8 us -> 24.8 us
  waiting for transfers between devices: 27 us -> 17.8 us
  starting transfers between devices: 14.6 us -> 21 us
    all_to_all x1 -> x0, waiting for transfers between devices: 14 us -> none  [local(): lax.all_to_all(gated, 'ctx', split_axis=0, concat_axis=1, tiled=True)]
    ppermute x0 -> x7, starting transfers between devices: none -> 13.6 us  [exchange_directly(): lax.ppermute(sent, axis, [(i, (i + step) % size) for i in range(size)])]
    dynamic_update_slice x16, other arithmetic: 11.5 us -> 1.36 us  [long_conv(): lax.map(one_block, (gated.reshape(count, block, length), filters.reshape(...]
    all_to_all x1 -> x0, starting transfers between devices: 7.94 us -> none  [local(): lax.all_to_all(gated, 'ctx', split_axis=0, concat_axis=1, tiled=True)]
    ppermute x0 -> x7, waiting for transfers between devices: none -> 4.48 us  [exchange_directly(): lax.ppermute(sent, axis, [(i, (i + step) % size) for i in range(size)])]
  transfers between devices with their start and end apart: 3 -> 9, of which waited for: 3 -> 5; matrix products, arithmetic and copies ran while one was open for 2% -> 2% of each run, Pallas kernels for 0% -> 0%
where the time goes in v1:
time: 257 us; the launch traced here: 256 us
  matrix products  165 us (64%)
  other arithmetic  24.8 us (10%)
  local copies, waits for them, and re-layouts  24 us (9%)
  starting transfers between devices  21 us (8%)
  waiting for transfers between devices  17.8 us (7%)
  loops' own time  3.65 us (1%)
    dot_general x32, matrix products, forward(): jnp.einsum('ckb,bm->ckm', twist_re, sin_cols, precision=HIGH)  20.2 us
    dot_general x32, matrix products, forward(): jnp.einsum('ckb,bm->ckm', twist_im, sin_cols, precision=HIGH)  19.8 us
    dot_general x32, matrix products, forward(): jnp.einsum('ckb,bm->ckm', twist_im, cos_cols, precision=HIGH)  19.5 us
    dot_general x32, matrix products, forward(): jnp.einsum('ckb,bm->ckm', twist_re, cos_cols, precision=HIGH)  19.5 us
    dot_general x64, matrix products, first_section(): jnp.einsum('ka,cab->ckb', table_rest, shaped, preferred_element_type=jnp....  17.9 us
    dot_general x64, matrix products, first_section(): jnp.einsum('ka,cab->ckb', table_head, shaped, preferred_element_type=jnp....  17.5 us
    while x48, local copies, waits for them, and re-layouts  14 us
    ppermute x7, starting transfers between devices, exchange_directly(): lax.ppermute(sent, axis, [(i, (i + step) % size) for i in range(size)])  13.6 us
  transfers between devices with their start and end apart: 9, of which 5 were waited for; matrix products, arithmetic and copies ran while one was open for 2% of the time, Pallas kernels for 0%

profile of v1, /device:TPU:0, one launch (start us, length us, event | category | flops | bytes accessed | tf_op | source)
XLA Modules:
  0.0 256.1 jit_solution(846500179866727178)
XLA Ops:
  0.0 1.3 slice.190
  1.6 1.3 slice.191
  3.5 2.4 collective-permute-start
  6.2 0.7 collective-permute-done
  7.5 1.3 maximum_convert_fusion.1
  8.8 11.1 %fusion.204 = bf16[2048,256]{1,0:T(8,128)(2,1)S(1)} fusion(f32[2048,262]{1,0:T(8,128)S(1)} %get-tuple-element.296, f32[2048,262]{1,0:T(8,128)S(1)} %get-tuple-element.295, f32[2048]{0:T(1024)S(1)} %bitcast.278, f32[2048]{0:T(1024)S(1)} %bitcast.277, f32[2048]{0:T(1024)S(1)} %bitcast.266, f32[2048]{0:T(1024)S(1)} %bitcast.267, f32[2048]{0:T(1024)S(1)} %bitcast.268, ...), kind=kLoop, calls=%fused_computation.204 | loop fusion | flops 14680064 | bytes 30523392 | tf_op jit(solution)/shard_map/convert_element_type | solution.py:148
  20.0 3.3 %collective-permute-start.1 = (bf16[256,256]{1,0:T(8,128)(2,1)S(1)}, bf16[256,256]{1,0:T(8,128)(2,1)S(1)}, u32[]{:S(2)}, u32[]{:S(2)}) collective-permute-start(bf16[256,256]{1,0:T(8,128)(2,1)S(1)} %get-tuple-element.269), channel_id=1, source_target_pairs={{0,4},{4,8},{8,12},{12,16},{16,20},{20,24},{24,28},{28,0},{1,5},{5... | collective-permute-start | bytes 393224 | tf_op jit(solution)/shard_map/ppermute | solution.py:28
  24.6 2.4 collective-permute-start.2
  26.9 2.4 collective-permute-start.3
  29.8 0.7 collective-permute-start.5
  30.5 1.8 collective-permute-start.6
  32.3 2.6 %collective-permute-start.7 = (bf16[256,256]{1,0:T(8,128)(2,1)S(1)}, bf16[256,256]{1,0:T(8,128)(2,1)S(1)}, u32[]{:S(2)}, u32[]{:S(2)}) collective-permute-start(bf16[256,256]{1,0:T(8,128)(2,1)S(1)} %get-tuple-element.263), channel_id=1, source_target_pairs={{0,28},{4,0},{8,4},{12,8},{16,12},{20,16},{24,20},{28,24},{1,29},{... | collective-permute-start | bytes 393224 | tf_op jit(solution)/shard_map/ppermute | solution.py:28
  34.9 0.9 collective-permute-done.3
  35.8 1.3 collective-permute-done.4
  37.1 2.2 collective-permute-done.5
  41.2 185.5 %while.12 = (s32[]{:T(128)}, bf16[16,16,2048]{2,1,0:T(8,128)(2,1)S(1)}, bf16[16,16,2048]{2,1,0:T(8,128)(2,1)S(1)}, bf16[16,16,2048]{2,1,0:T(8,128)(2,1)}, f32[16,16]{1,0:T(8,128)S(1)}, /*index=5*/s32[]{:T(128)}) while((s32[]{:T(128)}, bf16[16,16,2048]{2,1,0:T(8,128)(2,1)S(1)}, bf16[16,16,2048]{2,1,0:T(8,128)(2,1)S(1)}, ...), condition=%wide.region_1.2_spmd.clone.clone, body=%wide.region_0.1_spmd.clone.clone.sunk | while | flops 1256058880 | bytes 17597136 | solution.py:118
  41.2 0.9 dynamic-slice_bitcast_fusion.10
  43.9 0.6 convolution_add_fusion.11
  48.8 0.7 multiply_subtract_fusion.16
  52.8 0.9 dynamic-slice_bitcast_fusion.10
  55.5 0.6 convolution_add_fusion.11
  60.4 0.7 multiply_subtract_fusion.16
  64.4 0.9 dynamic-slice_bitcast_fusion.10
  67.1 0.6 convolution_add_fusion.11
  72.0 0.7 multiply_subtract_fusion.16
  76.0 0.9 dynamic-slice_bitcast_fusion.10
  78.7 0.6 convolution_add_fusion.11
  83.6 0.7 multiply_subtract_fusion.16
  87.6 0.9 dynamic-slice_bitcast_fusion.10
  90.3 0.6 convolution_add_fusion.11
  95.2 0.7 multiply_subtract_fusion.16
  99.2 0.9 dynamic-slice_bitcast_fusion.10
  101.9 0.6 convolution_add_fusion.11
  106.8 0.7 multiply_subtract_fusion.16
  110.8 0.9 dynamic-slice_bitcast_fusion.10
  113.5 0.6 convolution_add_fusion.11
  118.4 0.7 multiply_subtract_fusion.16
  122.4 0.9 dynamic-slice_bitcast_fusion.10
  125.1 0.6 convolution_add_fusion.11
  130.0 0.7 multiply_subtract_fusion.16
  134.0 0.9 dynamic-slice_bitcast_fusion.10
  141.6 0.7 multiply_subtract_fusion.16
  145.6 0.9 dynamic-slice_bitcast_fusion.10
  153.2 0.7 multiply_subtract_fusion.16
  157.2 0.9 dynamic-slice_bitcast_fusion.10
  164.7 0.7 multiply_subtract_fusion.16
  168.7 0.9 dynamic-slice_bitcast_fusion.10
  176.3 0.7 multiply_subtract_fusion.16
  180.3 0.9 dynamic-slice_bitcast_fusion.10
  183.1 0.6 convolution_add_fusion.11
  187.9 0.7 multiply_subtract_fusion.16
  191.9 0.9 dynamic-slice_bitcast_fusion.10
  199.5 0.7 multiply_subtract_fusion.16
  203.5 0.9 dynamic-slice_bitcast_fusion.10
  206.2 0.6 convolution_add_fusion.11
  211.1 0.7 multiply_subtract_fusion.16
  215.1 0.9 dynamic-slice_bitcast_fusion.10
  222.7 0.7 multiply_subtract_fusion.16
  227.0 1.2 copy.18
  228.2 5.0 %all-to-all-start = ((bf16[256,8,256]{2,0,1:T(8,128)(2,1)}), bf16[256,8,256]{2,0,1:T(8,128)(2,1)}, u32[]{:S(2)}, u32[]{:S(2)}) async-start(bf16[256,8,256]{2,0,1:T(8,128)(2,1)} %copy.18), calls=%async_computation | async-start | bytes 2097152 | tf_op jit(solution)/shard_map/all_to_all | solution.py:151
  233.2 1.1 copy.14
  234.3 2.0 maximum_convert_fusion
  236.3 12.6 %all-to-all-done = bf16[256,8,256]{2,0,1:T(8,128)(2,1)} async-done(((bf16[256,8,256]{2,0,1:T(8,128)(2,1)}), bf16[256,8,256]{2,0,1:T(8,128)(2,1)}, u32[]{:S(2)}, u32[]{:S(2)}) %all-to-all-start) | async-done | bytes 1048608 | tf_op jit(solution)/shard_map/all_to_all | solution.py:151
  248.9 7.2 %fusion.223 = bf16[2048,256]{1,0:T(8,128)(2,1)} fusion(f32[2048,262]{1,0:T(8,128)S(1)} %maximum_convert_fusion, f32[2048]{0:T(1024)S(1)} %bitcast.258, f32[2048]{0:T(1024)S(1)} %bitcast.259, f32[2048]{0:T(1024)S(1)} %bitcast.260, f32[2048]{0:T(1024)S(1)} %bitcast.261, f32[2048]{0:T(1024)S(1)} %bitcast.262, f32[2048]{0:T(1024)S(1)} %bitcast.263, ...), kind=kLoop, calls=%fused_computation.244 | loop fusion | flops 9437184 | bytes 16834560 | tf_op jit(solution)/shard_map/convert_element_type | solution.py:130
  (463 shorter events, 157.2 us)
Async XLA Ops:
  0.0 3.1 %copy-start = (bf16[2048,256]{1,0:T(8,128)(2,1)S(1)}, bf16[2048,256]{1,0:T(8,128)(2,1)}, u32[]{:S(2)}) copy-start(bf16[2048,256]{1,0:T(8,128)(2,1)} %param.10) | copy-start | bytes 3145732
  1.3 4.6 %copy-start.2 = (f32[3,7,2048]{2,1,0:T(8,128)S(1)}, f32[3,7,2048]{2,1,0:T(8,128)}, u32[]{:S(2)}) copy-start(f32[3,7,2048]{2,1,0:T(8,128)} %param.11) | copy-start | bytes 516100
  2.8 4.7 %copy-start.1 = (bf16[2048,256]{1,0:T(8,128)(2,1)S(1)}, bf16[2048,256]{1,0:T(8,128)(2,1)}, u32[]{:S(2)}) copy-start(bf16[2048,256]{1,0:T(8,128)(2,1)} %param.9) | copy-start | bytes 3145732
  3.5 3.3 %collective-permute-start = (bf16[3,2048,6]{1,2,0:T(8,128)(2,1)S(1)}, bf16[3,2048,6]{1,2,0:T(8,128)(2,1)S(1)}, u32[]{:S(2)}, u32[]{:S(2)}) collective-permute-start(bf16[3,2048,6]{1,2,0:T(8,128)(2,1)S(1)} %pad_maximum_fusion), channel_id=1, source_target_pairs={{0,4},{4,8},{8,12},{12,16},{16,20},{20,24},{24,28},{1,5},{5,9},{9,... | collective-permute-start | bytes 221192 | tf_op jit(solution)/shard_map/ppermute | solution.py:36
  19.9 4.0 %copy-start.3 = (f32[1,256]{1,0:T(1,128)S(1)}, f32[1,256]{1,0:T(1,128)}, u32[]{:S(2)}) copy-start(f32[1,256]{1,0:T(1,128)} %param.13) | copy-start | bytes 3076
  20.0 10.5 %collective-permute-start.1 = (bf16[256,256]{1,0:T(8,128)(2,1)S(1)}, bf16[256,256]{1,0:T(8,128)(2,1)S(1)}, u32[]{:S(2)}, u32[]{:S(2)}) collective-permute-start(bf16[256,256]{1,0:T(8,128)(2,1)S(1)} %get-tuple-element.269), channel_id=1, source_target_pairs={{0,4},{4,8},{8,12},{12,16},{16,20},{20,24},{24,28},{28,0},{1,5},{5... | collective-permute-start | bytes 393224 | tf_op jit(solution)/shard_map/ppermute | solution.py:28
  24.6 7.7 %collective-permute-start.2 = (bf16[256,256]{1,0:T(8,128)(2,1)S(1)}, bf16[256,256]{1,0:T(8,128)(2,1)S(1)}, u32[]{:S(2)}, u32[]{:S(2)}) collective-permute-start(bf16[256,256]{1,0:T(8,128)(2,1)S(1)} %get-tuple-element.268), channel_id=1, source_target_pairs={{0,8},{4,12},{8,16},{12,20},{16,24},{20,28},{24,0},{28,4},{1,9},{5... | collective-permute-start | bytes 393224 | tf_op jit(solution)/shard_map/ppermute | solution.py:28
  26.9 8.9 %collective-permute-start.3 = (bf16[256,256]{1,0:T(8,128)(2,1)S(1)}, bf16[256,256]{1,0:T(8,128)(2,1)S(1)}, u32[]{:S(2)}, u32[]{:S(2)}) collective-permute-start(bf16[256,256]{1,0:T(8,128)(2,1)S(1)} %get-tuple-element.267), channel_id=1, source_target_pairs={{0,12},{4,16},{8,20},{12,24},{16,28},{20,0},{24,4},{28,8},{1,13},{... | collective-permute-start | bytes 393224 | tf_op jit(solution)/shard_map/ppermute | solution.py:28
  29.3 7.8 %collective-permute-start.4 = (bf16[256,256]{1,0:T(8,128)(2,1)S(1)}, bf16[256,256]{1,0:T(8,128)(2,1)S(1)}, u32[]{:S(2)}, u32[]{:S(2)}) collective-permute-start(bf16[256,256]{1,0:T(8,128)(2,1)S(1)} %get-tuple-element.266), channel_id=1, source_target_pairs={{0,16},{4,20},{8,24},{12,28},{16,0},{20,4},{24,8},{28,12},{1,17},{... | collective-permute-start | bytes 393224 | tf_op jit(solution)/shard_map/ppermute | solution.py:28
  29.8 9.5 %collective-permute-start.5 = (bf16[256,256]{1,0:T(8,128)(2,1)S(1)}, bf16[256,256]{1,0:T(8,128)(2,1)S(1)}, u32[]{:S(2)}, u32[]{:S(2)}) collective-permute-start(bf16[256,256]{1,0:T(8,128)(2,1)S(1)} %get-tuple-element.265), channel_id=1, source_target_pairs={{0,20},{4,24},{8,28},{12,0},{16,4},{20,8},{24,12},{28,16},{1,21},{... | collective-permute-start | bytes 393224 | tf_op jit(solution)/shard_map/ppermute | solution.py:28
  30.5 8.9 %collective-permute-start.6 = (bf16[256,256]{1,0:T(8,128)(2,1)S(1)}, bf16[256,256]{1,0:T(8,128)(2,1)S(1)}, u32[]{:S(2)}, u32[]{:S(2)}) collective-permute-start(bf16[256,256]{1,0:T(8,128)(2,1)S(1)} %get-tuple-element.264), channel_id=1, source_target_pairs={{0,24},{4,28},{8,0},{12,4},{16,8},{20,12},{24,16},{28,20},{1,25},{... | collective-permute-start | bytes 393224 | tf_op jit(solution)/shard_map/ppermute | solution.py:28
  32.3 7.1 %collective-permute-start.7 = (bf16[256,256]{1,0:T(8,128)(2,1)S(1)}, bf16[256,256]{1,0:T(8,128)(2,1)S(1)}, u32[]{:S(2)}, u32[]{:S(2)}) collective-permute-start(bf16[256,256]{1,0:T(8,128)(2,1)S(1)} %get-tuple-element.263), channel_id=1, source_target_pairs={{0,28},{4,0},{8,4},{12,8},{16,12},{20,16},{24,20},{28,24},{1,29},{... | collective-permute-start | bytes 393224 | tf_op jit(solution)/shard_map/ppermute | solution.py:28
  228.2 20.7 %all-to-all-start = ((bf16[256,8,256]{2,0,1:T(8,128)(2,1)}), bf16[256,8,256]{2,0,1:T(8,128)(2,1)}, u32[]{:S(2)}, u32[]{:S(2)}) async-start(bf16[256,8,256]{2,0,1:T(8,128)(2,1)} %copy.18), calls=%async_computation | async-start | bytes 2097152 | tf_op jit(solution)/shard_map/all_to_all | solution.py:151
